TPU v7x, 512 devices: a whole 4x8x8 slice. The times are simulated.
512 devices in a mesh: limb: 16 (over x_hi, z), coef: 32 (over x_lo, y, core).
Axes of the slice: x: 4 (x_hi: 2, x_lo: 2; x = x_hi * 2 + x_lo), y: 8, z: 8, core: 2. Of those that a mesh axis runs over, the one named last changes fastest.
Arguments:
- cipher_zero: float32 [24, 32, 65536], P(None, 'limb', 'coef'), may hold values from -6 to 6
- cipher_one: float32 [24, 32, 65536], P(None, 'limb', 'coef'), may hold values from -6 to 6
- key_main: bfloat16 [24, 2, 2, 32, 65536], P(None, None, None, 'limb', 'coef'), may hold values from -5 to 5
- key_special: bfloat16 [24, 2, 2, 16, 65536], P(None, None, None, 'limb', 'coef'), may hold values from -5 to 5
- lift_main: float32 [32, 32], replicated, may hold values from -1.5 to 1.5
- lift_special: float32 [32, 16], replicated, may hold values from -1.5 to 1.5
- lower_table: float32 [16, 32], replicated, may hold values from -1.5 to 1.5
- inverse_scale: float32 [32], P('limb'), may hold values from 0.5 to 1.5
- inverse_main: float32 [32, 256, 256], P('limb', 'coef'), may hold values from 0.5 to 1.5
- inverse_special: float32 [16, 256, 256], P('limb', 'coef'), may hold values from 0.5 to 1.5
- forward_main: float32 [32, 256, 256], P('limb', 'coef'), may hold values from 0.5 to 1.5
- forward_special: float32 [16, 256, 256], P('limb', 'coef'), may hold values from 0.5 to 1.5
- inverse_rows: float32 [256, 256], replicated, may hold values from -0.375 to 0.375
- inverse_columns: float32 [256, 256], replicated, may hold values from -0.375 to 0.375
- forward_rows: float32 [256, 256], replicated, may hold values from -0.375 to 0.375
- forward_columns: float32 [256, 256], replicated, may hold values from -0.375 to 0.375
Outputs:
- switched_zero: float32 [24, 32, 65536], P(None, 'limb', 'coef')
- switched_one: float32 [24, 32, 65536], P(None, 'limb', 'coef')
All inputs are finite; a program needn't handle non-finite values.
Results may differ from a plain program's by a relative error of at most 0.0003.
Values sent between devices are 32-bit elements; how exact they have to be, the bound alone decides.
A program may use at most 64 MiB of HBM per device.

v0:
```python
import functools

import jax
import jax.numpy as jnp
from jax import lax
from jax.experimental import pallas as pl
from jax.experimental.pallas import tpu as pltpu
from jax.sharding import PartitionSpec as P

F32, BF16 = jnp.float32, jnp.bfloat16
HIGHEST = lax.Precision.HIGHEST
MESH = pl.DeviceIdType.MESH
ROWS = COLS = 256
SUB, LANE = 8, 128
PART = 8
ORDER_SKEW = 1.0


def halves(v):
    high = v.astype(BF16)
    return high, (v - high.astype(F32)).astype(BF16)


def iota(shape, axis):
    return lax.broadcasted_iota(jnp.int32, shape, axis)


def selector(shape, condition):
    return jnp.where(condition(iota(shape, 0), iota(shape, 1)), 1.0, 0.0).astype(F32)


def exact(a, b, dims):
    return lax.dot_general(a, b, (dims, ((), ())), precision=HIGHEST, preferred_element_type=F32)


def fold(a, b):
    return jnp.dot(a, b, preferred_element_type=F32)


def data_rows(v):
    high, low = halves(v)
    return jnp.concatenate([high, high, low], axis=1)


def data_columns(v):
    high, low = halves(v)
    return jnp.concatenate([high, high, low], axis=0)


def weight_right(v):
    high, low = halves(v)
    return jnp.concatenate([high, low, high], axis=0)


def weight_left(v):
    high, low = halves(v)
    return jnp.concatenate([high, low, high], axis=1)


def kernel(
    coef_size, limb_size, chunks,
    x_ref, zero_ref, km_ref, ks_ref, lift_main_ref, lift_special_ref, lower_ref, scale_ref,
    tim_ref, tis_ref, tfm_ref, tfs_ref, ir_ref, ic_ref, fr_ref, fc_ref,
    out0_ref, out1_ref,
    send1, got1, send2, got2, got3, send4, got4, send5, got5, send6, got6, got7, send8, got8,
    send_t, got_t, twist, total, ic_w, fc_w, m_w, lift_w, lower_w,
    ssem, rsem, tsem,
):
    coef = lax.axis_index("coef")
    limb = lax.axis_index("limb")
    ring = limb_size // 2
    side = limb // ring
    place = lax.rem(limb, ring)

    barrier = pltpu.get_barrier_semaphore()

    @pl.loop(1, coef_size)
    def _(j):
        pl.semaphore_signal(barrier, inc=1, device_id={"coef": lax.rem(coef + j, coef_size)}, device_id_type=MESH)

    @pl.loop(1, limb_size)
    def _(j):
        pl.semaphore_signal(barrier, inc=1, device_id={"limb": lax.rem(limb + j, limb_size)}, device_id_type=MESH)

    def push(source, target, axis, peer, stage, g):
        pltpu.make_async_remote_copy(
            src_ref=source, dst_ref=target, send_sem=ssem.at[stage, g], recv_sem=rsem.at[stage, g],
            device_id={axis: peer}, device_id_type=MESH,
        ).start()

    def settle(ref, sem):
        pltpu.make_async_copy(ref, ref, sem).wait()

    def coef_push(send, got, stage, g):
        @pl.loop(1, coef_size)
        def _(j):
            peer = lax.rem(coef + j, coef_size)
            push(send.at[g, peer], got.at[g, coef], "coef", peer, stage, g)

        got[g, coef] = send[g, coef]

    def coef_wait(got, stage, g):
        settle(got.at[g, pl.ds(0, coef_size - 1)], rsem.at[stage, g])

    def to_items(ref, g, v):
        for n in range(v.shape[0]):
            for h in range(2):
                ref[g, 2 * n + h] = v[n, :, h * LANE:(h + 1) * LANE]

    def stage1(g):
        v = x_ref[pl.ds(PART * g, PART)].reshape(PART * 2 * SUB, COLS)
        a = fold(data_rows(v), ic_w[...]).reshape(PART, 2, SUB, COLS) * tim_ref[...][None]
        to_items(send1, g, a.reshape(PART * 2, SUB, COLS))

    def push1(g):
        coef_push(send1, got1, 0, g)

    def stage2(g):
        coef_wait(got1, 0, g)
        v = got1[g].reshape(ROWS, LANE)
        send2[g] = fold(m_w[...], data_columns(v)).reshape(coef_size, SUB, LANE)
        coef_push(send2, got2, 1, g)

    def stage3(g):
        coef_wait(got2, 1, g)

        @pl.loop(1, ring)
        def _(j):
            to = lax.rem(place + j, ring)
            push(got2.at[g, pl.ds(4 * to, 4)], got3.at[g, place], "limb", side * ring + to, 2, g)

        got3[g, place] = got2[g, pl.ds(4 * place, 4)]

    def mixed(weight, got, send, stage, per, g, wait_count, wait_stage):
        settle(got.at[g, pl.ds(0, wait_count)], rsem.at[wait_stage, g])
        v = got[g].reshape(limb_size, 2, SUB, LANE)
        both = jnp.concatenate(
            [v[:, 0].reshape(limb_size * SUB, LANE), v[:, 1].reshape(limb_size * SUB, LANE)], axis=1
        )
        w = fold(weight[...], data_columns(both)).reshape(limb_size, per, SUB, 2 * LANE)
        for h in range(2):
            send[g, :, :, h] = w[..., h * LANE:(h + 1) * LANE]

    def limb_push(send, got, stage, g):
        @pl.loop(1, limb_size)
        def _(j):
            peer = lax.rem(limb + j, limb_size)
            push(send.at[g, peer], got.at[g, limb], "limb", peer, stage, g)

        got[g, limb] = send[g, limb]

    def stage4(g):
        mixed(lift_w, got3, send4, 3, 3, g, ring - 1, 2)
        limb_push(send4, got4, 3, g)

    def finish(v, kinds, n):
        parts = [(v[:, :, h] * twist[:kinds, h][None]).reshape(n * kinds * SUB, LANE) for h in range(2)]
        rows = jnp.concatenate(parts, axis=1)
        return fold(data_rows(rows), fc_w[...]).reshape(n, kinds * SUB, COLS)

    def stage5(g):
        settle(got4.at[g, pl.ds(0, limb_size - 1)], rsem.at[3, g])
        values = finish(got4[g], 3, limb_size).reshape(2, PART, 3 * SUB, COLS)
        here = pl.ds(PART * g, PART)
        for i in range(2):
            total[g, :, i] = sum(
                values[d, :, :2 * SUB] * km_ref[here, d, i].astype(F32) for d in range(2)
            )
        special = 0.0
        for d in range(2):
            v = values[d, :, 2 * SUB:]
            special = special + jnp.concatenate([v, v], axis=1) * ks_ref[here, d].astype(F32)
        a = fold(data_rows(special.reshape(PART * 2 * SUB, COLS)), ic_w[...])
        a = a.reshape(PART * 2, SUB, COLS) * tis_ref[...]
        to_items(send5, g, a)
        coef_push(send5, got5, 4, g)

    def stage6(g):
        coef_wait(got5, 4, g)
        v = got5[g].reshape(ROWS, LANE)
        send6[g] = fold(m_w[...], data_columns(v)).reshape(coef_size, SUB, LANE)
        coef_push(send6, got6, 5, g)

    def stage7(g):
        coef_wait(got6, 5, g)

        @pl.loop(1, limb_size)
        def _(j):
            to = lax.rem(limb + j, limb_size)
            push(got6.at[g, pl.ds(2 * to, 2)], got7.at[g, limb], "limb", to, 6, g)

        got7[g, limb] = got6[g, pl.ds(2 * limb, 2)]

    def stage8(g):
        mixed(lower_w, got7, send8, 7, 2, g, limb_size - 1, 6)
        limb_push(send8, got8, 7, g)

    def stage9(g):
        settle(got8.at[g, pl.ds(0, limb_size - 1)], rsem.at[7, g])
        low = finish(got8[g], 2, limb_size).reshape(PART, 2, 2, SUB, COLS)
        here = pl.ds(PART * g, PART)
        for t in range(2):
            for i, out in enumerate((out0_ref, out1_ref)):
                result = scale_ref[t] * (total[g, :, i, t * SUB:(t + 1) * SUB] - low[:, i, t])
                out[here, t] = zero_ref[here, t] + result if i == 0 else result

    def prepare_twist():
        rows = jnp.concatenate(
            [tfm_ref[...].reshape(2 * SUB, ROWS), tfs_ref[...].reshape(SUB, ROWS), jnp.zeros((LANE - 3 * SUB, ROWS), F32)],
            axis=0,
        )
        send_t[...] = rows.T.reshape(coef_size, SUB, LANE)

    def push_twist():
        @pl.loop(1, coef_size)
        def _(j):
            peer = lax.rem(coef + j, coef_size)
            pltpu.make_async_remote_copy(
                src_ref=send_t.at[peer], dst_ref=got_t.at[coef], send_sem=tsem.at[0], recv_sem=tsem.at[1],
                device_id={"coef": peer}, device_id_type=MESH,
            ).start()

        got_t[coef] = send_t[coef]

    def build_twist():
        settle(got_t.at[pl.ds(0, coef_size - 1)], tsem.at[1])
        lanes = iota((SUB, LANE), 1) // SUB
        per = LANE // SUB
        for t in range(3):
            for h in range(2):
                value = jnp.zeros((SUB, LANE), F32)
                for q in range(per):
                    tile = got_t[h * per + q]
                    shift = (q - t) * SUB % LANE
                    moved = pltpu.roll(tile, shift, 1) if shift else tile
                    value = jnp.where(lanes == q, moved, value)
                twist[t, h] = value

    def build_weights():
        m_w[...] = weight_left(exact(fr_ref[...], ir_ref[...], ((0,), (1,))))
        fc_w[...] = weight_right(fc_ref[...])

    def build_mixes():
        depth = limb_size * SUB
        spread = selector((limb_size, depth), lambda s, c: c // SUB == s)
        mine = pl.ds(pl.multiple_of(side * limb_size, SUB), limb_size)

        def expand(table, rows):
            wide = exact(table, spread, ((1,), (0,)))
            keep = lax.rem(iota((rows, depth), 0), SUB) == lax.rem(iota((rows, depth), 1), SUB)
            return weight_left(jnp.where(keep, wide, 0.0))

        rows = limb_size * 3 * SUB
        kinds = limb_size * 2

        def main_of(r, t):
            which = r // SUB
            return (lax.rem(which, 3) < 2) & (2 * (which // 3) + lax.rem(which, 3) == t)

        def special_of(r, u):
            which = r // SUB
            return (lax.rem(which, 3) == 2) & (which // 3 == u)

        table = exact(selector((rows, kinds), main_of), lift_main_ref[mine], ((1,), (1,)))
        table = table + exact(selector((rows, limb_size), special_of), lift_special_ref[mine], ((1,), (1,)))
        lift_w[...] = expand(table, rows)
        rows = kinds * SUB
        table = exact(selector((rows, kinds), lambda r, t: r // SUB == t), lower_ref[...], ((1,), (1,)))
        lower_w[...] = expand(table, rows)

    ic_w[...] = weight_right(ic_ref[...])
    stage1(0)
    pl.semaphore_wait(barrier, coef_size + limb_size - 2)
    push1(0)
    build_weights()
    prepare_twist()
    for g in range(1, chunks):
        stage1(g)
        push1(g)
    push_twist()
    build_mixes()
    work = []
    for g in range(chunks):
        for k, step in enumerate((stage2, stage3, stage4, stage5, stage6, stage7, stage8, stage9)):
            work.append((k + ORDER_SKEW * g, g, k, step))
    work.sort(key=lambda w: w[:3])
    twisted = False
    for _, g, k, step in work:
        if k >= 2 and not twisted:
            build_twist()
            twisted = True
        step(g)

    for g in range(chunks):
        for stage, ref, count in (
            (0, got1, coef_size - 1), (1, got2, coef_size - 1), (2, got3, ring - 1), (3, got4, limb_size - 1),
            (4, got5, coef_size - 1), (5, got6, coef_size - 1), (6, got7, limb_size - 1), (7, got8, limb_size - 1),
        ):
            settle(ref.at[g, pl.ds(0, count)], ssem.at[stage, g])
    settle(got_t.at[pl.ds(0, coef_size - 1)], tsem.at[0])


def on_device(
    coef_size, limb_size,
    cipher_zero, cipher_one, key_main, key_special, lift_main, lift_special, lower_table, inverse_scale,
    inverse_main, inverse_special, forward_main, forward_special,
    inverse_rows, inverse_columns, forward_rows, forward_columns,
):
    ciphers = cipher_one.shape[0]
    chunks = ciphers // PART
    tile = (SUB, LANE)
    vmem = pl.BlockSpec(memory_space=pltpu.VMEM)
    smem = pl.BlockSpec(memory_space=pltpu.SMEM)
    out = jax.ShapeDtypeStruct((ciphers, 2, SUB, COLS), F32)
    item = pltpu.VMEM((chunks, coef_size) + tile, F32)
    depth = limb_size * SUB
    stages = 8
    zero, one = pl.pallas_call(
        functools.partial(kernel, coef_size, limb_size, chunks),
        out_shape=(out, out),
        in_specs=[vmem] * 7 + [smem] + [vmem] * 8,
        out_specs=(vmem, vmem),
        scratch_shapes=[
            item, item, item, item,
            pltpu.VMEM((chunks, limb_size // 2, 4) + tile, F32),
            pltpu.VMEM((chunks, limb_size, 3, 2) + tile, F32),
            pltpu.VMEM((chunks, limb_size, 3, 2) + tile, F32),
            item, item, item, item,
            pltpu.VMEM((chunks, limb_size, 2) + tile, F32),
            pltpu.VMEM((chunks, limb_size, 2, 2) + tile, F32),
            pltpu.VMEM((chunks, limb_size, 2, 2) + tile, F32),
            pltpu.VMEM((coef_size,) + tile, F32),
            pltpu.VMEM((coef_size,) + tile, F32),
            pltpu.VMEM((3, 2) + tile, F32),
            pltpu.VMEM((chunks, PART, 2, 2 * SUB, COLS), F32),
            pltpu.VMEM((3 * COLS, COLS), BF16),
            pltpu.VMEM((3 * COLS, COLS), BF16),
            pltpu.VMEM((ROWS, 3 * ROWS), BF16),
            pltpu.VMEM((3 * depth, 3 * depth), BF16),
            pltpu.VMEM((2 * depth, 3 * depth), BF16),
            pltpu.SemaphoreType.DMA((stages, chunks)),
            pltpu.SemaphoreType.DMA((stages, chunks)),
            pltpu.SemaphoreType.DMA((2,)),
        ],
        compiler_params=pltpu.CompilerParams(
            collective_id=0, has_side_effects=True, vmem_limit_bytes=40 << 20
        ),
    )(
        cipher_one.reshape(ciphers, 2, SUB, COLS),
        cipher_zero.reshape(ciphers, 2, SUB, COLS),
        key_main.reshape(ciphers, 2, 2, 2 * SUB, COLS),
        key_special.reshape(ciphers, 2, 2 * SUB, COLS),
        lift_main, lift_special, lower_table, inverse_scale,
        inverse_main, inverse_special, forward_main, forward_special,
        inverse_rows, inverse_columns, forward_rows, forward_columns,
    )
    return zero.reshape(cipher_zero.shape), one.reshape(cipher_one.shape)


def solution(mesh):
    spread = P(None, "limb", "coef")
    keys = P(None, None, None, "limb", "coef")
    local = P("limb", "coef", None)
    placed = (spread, spread, keys, keys, P(), P(), P(), P("limb"), local, local, local, local, P(), P(), P(), P())
    return jax.shard_map(
        functools.partial(on_device, mesh.shape["coef"], mesh.shape["limb"]),
        mesh=mesh,
        in_specs=placed,
        out_specs=(spread, spread),
        check_vma=False,
    )
```

profile of v0, /device:TPU:2, one launch (start us, length us, event | category | flops | bytes accessed | tf_op | source)
XLA Modules:
  0.0 129.0 jit_solution(14258574537008439957)
XLA Ops:
  0.6 0.8 copy.18.lift_special_ref
  1.4 0.0 copy-start.12
  1.4 0.0 copy-start.13
  1.4 1.4 %reshape.23.zero_ref = f32[24,2,8,256]{3,2,1,0:T(8,128)S(1)} reshape(f32[24,2,2048]{2,1,0:T(2,128)} %param.16) | data formatting | bytes 786432 | tf_op jit(solution)/shard_map/reshape | solution.py:350
  2.8 0.0 copy-done.12
  2.8 0.0 copy-start.11
  2.8 0.3 reshape.22.x_ref
  3.1 0.0 copy-done.13
  3.1 0.3 reshape.25.ks_ref
  3.4 0.5 copy-done.11
  3.9 0.0 copy-start
  3.9 0.0 copy-start.1
  3.9 0.0 copy-start.2
  3.9 0.5 reshape.24.km_ref
  4.4 0.4 copy-done
  4.9 0.1 copy-done.1
  5.0 0.1 copy-done.2
  5.0 0.0 copy-start.3
  5.0 0.9 copy-done.3
  6.0 0.0 copy-start.4
  6.0 0.7 copy-done.4
  6.7 0.0 copy-start.5
  6.7 0.7 copy-done.5
  7.4 0.0 copy-start.6
  7.4 0.7 copy-done.6
  8.2 0.0 copy-start.7
  8.2 0.7 copy-done.7
  8.8 0.0 copy-start.8
  8.9 0.7 copy-done.8
  9.5 0.0 copy-start.9
  9.5 0.7 copy-done.9
  10.2 0.0 copy-start.10
  10.2 0.7 copy-done.10
  10.9 116.1 %shard_map.167 = (f32[24,2,8,256]{3,2,1,0:T(8,128)S(1)}, f32[24,2,8,256]{3,2,1,0:T(8,128)S(1)}) custom-call(f32[24,2,8,256]{3,2,1,0:T(8,128)S(1)} %reshape.22.x_ref, f32[24,2,8,256]{3,2,1,0:T(8,128)S(1)} %reshape.23.zero_ref, bf16[24,2,2,16,256]{4,3,2,1,0:T(8,128)(2,1)S(1)} %reshape.24.km_ref, bf16[24,2,16,256]{3,2,1,0:T(8,128)(2,1)S(1)} %reshape.25.ks_ref, ...), custom_call_target="tpu_custom_call" | custom-call | tf_op jit(solution)/shard_map/pallas_call | solution.py:318
  127.0 1.0 reshape.26
  128.0 1.0 reshape.27
Async XLA Ops:
  1.4 1.4 %copy-start.12 = (f32[24,2,2048]{2,1,0:T(2,128)S(1)}, f32[24,2,2048]{2,1,0:T(2,128)}, u32[]{:S(2)}) copy-start(f32[24,2,2048]{2,1,0:T(2,128)} %param.17) | copy-start | bytes 1179652
  1.4 1.7 %copy-start.13 = (bf16[24,2,2,1,2048]{4,2,3,1,0:T(2,128)(2,1)S(1)}, bf16[24,2,2,1,2048]{4,2,3,1,0:T(2,128)(2,1)}, u32[]{:S(2)}) copy-start(bf16[24,2,2,1,2048]{4,2,3,1,0:T(2,128)(2,1)} %param.19) | copy-start | bytes 1179652
  2.8 1.1 copy-start.11
  3.9 0.9 copy-start
  3.9 1.0 copy-start.1
  3.9 1.1 copy-start.2
  5.0 0.9 copy-start.3
  6.0 0.7 copy-start.4
  6.7 0.7 copy-start.5
  7.4 0.7 copy-start.6
  8.2 0.7 copy-start.7
  8.8 0.7 copy-start.8
  9.5 0.7 copy-start.9
  10.2 0.7 copy-start.10
where the time goes:
time: 130 us; the launch traced here: 129 us
  Pallas kernels  116 us (89%)
  local copies, waits for them, and re-layouts  12.2 us (9%)
    pallas_call x1, Pallas kernels, on_device(): pl.pallas_call(functools.partial(kernel, coef_size, limb_size, chunks), o...  116 us
    unnamed x29, local copies, waits for them, and re-layouts  7.76 us

commit v1 on v0

v1 whole, which is shorter than its diff:
```python
import functools

import jax
import jax.numpy as jnp
from jax import lax
from jax.experimental import pallas as pl
from jax.experimental.pallas import tpu as pltpu
from jax.sharding import PartitionSpec as P

F32, BF16 = jnp.float32, jnp.bfloat16
HIGHEST = lax.Precision.HIGHEST
MESH = pl.DeviceIdType.MESH
ROWS = COLS = 256
SUB, LANE = 8, 128
PART = 8
ORDER_SKEW = 0.0
SMALL = ("lift_main", "lift_special", "lower", "scale", "tim", "tis", "tfm", "tfs", "ir", "ic", "fr", "fc")


def halves(v):
    high = v.astype(BF16)
    return high, (v - high.astype(F32)).astype(BF16)


def iota(shape, axis):
    return lax.broadcasted_iota(jnp.int32, shape, axis)


def selector(shape, condition):
    return jnp.where(condition(iota(shape, 0), iota(shape, 1)), 1.0, 0.0).astype(F32)


def exact(a, b, dims):
    return lax.dot_general(a, b, (dims, ((), ())), precision=HIGHEST, preferred_element_type=F32)


def fold(a, b):
    return jnp.dot(a, b, preferred_element_type=F32)


def data_rows(v):
    high, low = halves(v)
    return jnp.concatenate([high, high, low], axis=1)


def data_columns(v):
    high, low = halves(v)
    return jnp.concatenate([high, high, low], axis=0)


def weight_right(v):
    high, low = halves(v)
    return jnp.concatenate([high, low, high], axis=0)


def weight_left(v):
    high, low = halves(v)
    return jnp.concatenate([high, low, high], axis=1)


def kernel(
    coef_size, limb_size, chunks,
    x_ref, zero_ref, km_ref, ks_ref, *rest,
):
    names = len(SMALL)
    sources, (out0_ref, out1_ref) = rest[:names], rest[names:names + 2]
    held, rest = rest[names + 2:2 * names + 2], rest[2 * names + 2:]
    lsem, rest = rest[0], rest[1:]
    loads = {
        name: pltpu.make_async_copy(source, target, lsem.at[n])
        for n, (name, source, target) in enumerate(zip(SMALL, sources, held))
    }
    for name in SMALL:
        loads[name].start()
    (lift_main_ref, lift_special_ref, lower_ref, scale_ref, tim_ref, tis_ref, tfm_ref, tfs_ref,
     ir_ref, ic_ref, fr_ref, fc_ref) = held
    body(coef_size, limb_size, chunks, loads, x_ref, zero_ref, km_ref, ks_ref,
         lift_main_ref, lift_special_ref, lower_ref, scale_ref, tim_ref, tis_ref, tfm_ref, tfs_ref,
         ir_ref, ic_ref, fr_ref, fc_ref, out0_ref, out1_ref, *rest)


def body(
    coef_size, limb_size, chunks, loads,
    x_ref, zero_ref, km_ref, ks_ref, lift_main_ref, lift_special_ref, lower_ref, scale_ref,
    tim_ref, tis_ref, tfm_ref, tfs_ref, ir_ref, ic_ref, fr_ref, fc_ref,
    out0_ref, out1_ref,
    send1, got1, send2, got3, send4, got4, send5, got5, send6, got7, send8, got8,
    send_t, got_t, twist, total, ic_w, fc_w, m_w, lift_w, lower_w,
    ssem, rsem, tsem,
):
    coef = lax.axis_index("coef")
    limb = lax.axis_index("limb")
    ring = limb_size // 2
    side = limb // ring
    place = lax.rem(limb, ring)
    core = lax.rem(coef, 2)
    chip = coef // 2
    tall = coef_size // 4
    height = lax.rem(chip, tall)

    barrier = pltpu.get_barrier_semaphore()

    @pl.loop(1, coef_size)
    def _(j):
        pl.semaphore_signal(barrier, inc=1, device_id={"coef": lax.rem(coef + j, coef_size)}, device_id_type=MESH)

    @pl.loop(1, limb_size)
    def _(j):
        pl.semaphore_signal(barrier, inc=1, device_id={"limb": lax.rem(limb + j, limb_size)}, device_id_type=MESH)

    def need(*which):
        for name in which:
            loads[name].wait()

    def push(source, target, peer, stage, g):
        pltpu.make_async_remote_copy(
            src_ref=source, dst_ref=target, send_sem=ssem.at[stage, g], recv_sem=rsem.at[stage, g],
            device_id=peer, device_id_type=MESH,
        ).start()

    def settle(ref, sem):
        pltpu.make_async_copy(ref, ref, sem).wait()

    def settle_back(got, sem, selfish):
        @pl.when(selfish)
        def _():
            settle(got.at[pl.ds(0, coef_size - 1)], sem)

        @pl.when(jnp.logical_not(selfish))
        def _():
            settle(got, sem)

    def coef_push(send, got, stage, g):
        @pl.loop(1, coef_size)
        def _(j):
            peer = lax.rem(coef + j, coef_size)
            push(send.at[g, peer], got.at[g, coef], {"coef": peer}, stage, g)

        got[g, coef] = send[g, coef]

    def coef_wait(got, stage, g):
        settle(got.at[g, pl.ds(0, coef_size - 1)], rsem.at[stage, g])

    def stage1(g):
        v = x_ref[pl.ds(PART * g, PART)].reshape(PART * 2 * SUB, COLS)
        a = fold(data_rows(v), ic_w[...]).reshape(PART, 2, SUB, COLS) * tim_ref[...][None]
        for b in range(PART):
            for h in range(2):
                for l in range(2):
                    send1[g, 4 * b + 2 * h + l] = a[b, l, :, h * LANE:(h + 1) * LANE]

    def push1(g):
        coef_push(send1, got1, 0, g)

    def rows_of(high, low):
        return high * tall + lax.rem(low + height, tall)

    def stage2(g):
        coef_wait(got1, 0, g)
        v = got1[g].reshape(ROWS, LANE)
        send2[g] = fold(m_w[...], data_columns(v)).reshape(coef_size, SUB, LANE)
        slot = 2 * place + core

        @pl.loop(1, limb_size)
        def _(j):
            to = lax.rem(slot + j, limb_size)
            low, high = to // 2, lax.rem(to, 2)
            push(
                send2.at[g, pl.ds(2 * rows_of(high, low), 2)], got3.at[g, slot],
                {"limb": side * ring + low, "coef": 2 * chip + high}, 1, g,
            )

        got3[g, slot] = send2[g, pl.ds(2 * rows_of(core, place), 2)]

    def mix_and_push(weight, got, wait_stage, send, back, stage, per, block, source, g):
        settle(got.at[g, pl.ds(0, limb_size - 1)], rsem.at[wait_stage, g])
        v = got[g]
        both = jnp.concatenate([v[:, u].reshape(limb_size * SUB, LANE) for u in range(2)], axis=1)
        w = fold(weight[...], data_columns(both)).reshape(limb_size, per, SUB, 2 * LANE)
        for u in range(2):
            send[g, :, u] = w[..., u * LANE:(u + 1) * LANE]

        @pl.loop(0, 2 * limb_size)
        def _(j):
            to = lax.rem(limb + j // 2, limb_size)
            u = lax.rem(core + j, 2)
            peer = 2 * block + u

            @pl.when((to != limb) | (peer != coef))
            def _():
                push(send.at[g, to, u], back.at[g, source], {"limb": to, "coef": peer}, stage, g)

        @pl.when(block == chip)
        def _():
            back[g, source] = send[g, limb, core]

    lift_block, lower_block = rows_of(core, place), rows_of(side, place)

    def stage3(g):
        mix_and_push(lift_w, got3, 1, send4, got4, 2, 3, lift_block, side * (coef_size // 2) + chip, g)

    def finish(v, kinds):
        n = v.shape[0]
        parts = [(v[:, h] * twist[:kinds, h][None]).reshape(n * kinds * SUB, LANE) for h in range(2)]
        rows = jnp.concatenate(parts, axis=1)
        return fold(data_rows(rows), fc_w[...]).reshape(n, kinds * SUB, COLS)

    def stage4(g):
        settle_back(got4.at[g], rsem.at[2, g], lift_block == chip)
        values = finish(got4[g].reshape(2 * PART, 2, 3, SUB, LANE), 3).reshape(2, PART, 3 * SUB, COLS)
        here = pl.ds(PART * g, PART)
        special = 0.0
        for d in range(2):
            v = values[d, :, 2 * SUB:]
            special = special + jnp.concatenate([v, v], axis=1) * ks_ref[here, d].astype(F32)
        a = fold(data_rows(special.reshape(PART * 2 * SUB, COLS)), ic_w[...])
        a = a.reshape(PART * 2, SUB, COLS) * tis_ref[...]
        for n in range(PART * 2):
            for h in range(2):
                send5[g, 2 * n + h] = a[n, :, h * LANE:(h + 1) * LANE]
        coef_push(send5, got5, 3, g)
        for i in range(2):
            total[g, :, i] = sum(
                values[d, :, :2 * SUB] * km_ref[here, d, i].astype(F32) for d in range(2)
            )

    def stage5(g):
        coef_wait(got5, 3, g)
        v = got5[g].reshape(ROWS, LANE)
        send6[g] = fold(m_w[...], data_columns(v)).reshape(coef_size, SUB, LANE)

        @pl.loop(1, limb_size)
        def _(j):
            to = lax.rem(limb + j, limb_size)
            rows = rows_of(to // ring, lax.rem(to, ring))
            push(send6.at[g, pl.ds(2 * rows, 2)], got7.at[g, limb], {"limb": to}, 4, g)

        got7[g, limb] = send6[g, pl.ds(2 * lower_block, 2)]

    def stage6(g):
        mix_and_push(lower_w, got7, 4, send8, got8, 5, 2, lower_block, coef, g)

    def stage7(g):
        settle_back(got8.at[g], rsem.at[5, g], lower_block == chip)
        low = finish(got8[g].reshape(2 * PART, 2, 2, SUB, LANE), 2).reshape(PART, 2, 2, SUB, COLS)
        here = pl.ds(PART * g, PART)
        for t in range(2):
            for i, out in enumerate((out0_ref, out1_ref)):
                result = scale_ref[t] * (total[g, :, i, t * SUB:(t + 1) * SUB] - low[:, i, t])
                out[here, t] = zero_ref[here, t] + result if i == 0 else result

    def prepare_twist():
        rows = jnp.concatenate(
            [tfm_ref[...].reshape(2 * SUB, ROWS), tfs_ref[...].reshape(SUB, ROWS), jnp.zeros((LANE - 3 * SUB, ROWS), F32)],
            axis=0,
        )
        send_t[...] = rows.T.reshape(coef_size, SUB, LANE)

    def push_twist():
        @pl.loop(1, coef_size)
        def _(j):
            peer = lax.rem(coef + j, coef_size)
            pltpu.make_async_remote_copy(
                src_ref=send_t.at[peer], dst_ref=got_t.at[coef], send_sem=tsem.at[0], recv_sem=tsem.at[1],
                device_id={"coef": peer}, device_id_type=MESH,
            ).start()

        got_t[coef] = send_t[coef]

    def build_twist():
        settle(got_t.at[pl.ds(0, coef_size - 1)], tsem.at[1])
        lanes = iota((SUB, LANE), 1) // SUB
        per = LANE // SUB
        for t in range(3):
            for h in range(2):
                value = jnp.zeros((SUB, LANE), F32)
                for q in range(per):
                    tile = got_t[h * per + q]
                    shift = (q - t) * SUB % LANE
                    moved = pltpu.roll(tile, shift, 1) if shift else tile
                    value = jnp.where(lanes == q, moved, value)
                twist[t, h] = value

    def build_weights():
        m_w[...] = weight_left(exact(fr_ref[...], ir_ref[...], ((0,), (1,))))
        fc_w[...] = weight_right(fc_ref[...])

    def build_mixes():
        depth = limb_size * SUB
        kinds = limb_size * 2

        def expand(table, spread):
            rows = table.shape[0]
            wide = exact(table, spread, ((1,), (0,)))
            keep = lax.rem(iota((rows, depth), 0), SUB) == lax.rem(iota((rows, depth), 1), SUB)
            return weight_left(jnp.where(keep, wide, 0.0))

        def main_of(r, t):
            which = r // SUB
            return (lax.rem(which, 3) < 2) & (2 * (which // 3) + lax.rem(which, 3) == t)

        def special_of(r, u):
            which = r // SUB
            return (lax.rem(which, 3) == 2) & (which // 3 == u)

        rows = limb_size * 3 * SUB
        table = exact(selector((rows, kinds), main_of), lift_main_ref[...], ((1,), (1,)))
        table = table + exact(selector((rows, limb_size), special_of), lift_special_ref[...], ((1,), (0,)))
        lift_w[...] = expand(table, selector((kinds, depth), lambda s, c: c // SUB + side * limb_size == s))
        table = exact(selector((kinds * SUB, kinds), lambda r, t: r // SUB == t), lower_ref[...], ((1,), (1,)))
        lower_w[...] = expand(table, selector((limb_size, depth), lambda s, c: c // SUB == s))

    need("ic", "tim")
    ic_w[...] = weight_right(ic_ref[...])
    stage1(0)
    pl.semaphore_wait(barrier, coef_size + limb_size - 2)
    push1(0)
    need("ir", "fr", "fc", "tfm", "tfs", "tis", "scale")
    build_weights()
    prepare_twist()
    for g in range(1, chunks):
        stage1(g)
        push1(g)
    push_twist()
    need("lift_main", "lift_special", "lower")
    build_mixes()
    work = []
    for g in range(chunks):
        for k, step in enumerate((stage2, stage3, stage4, stage5, stage6, stage7)):
            work.append((k + ORDER_SKEW * g, g, k, step))
    work.sort(key=lambda w: w[:3])
    twisted = False
    for _, g, k, step in work:
        if k >= 2 and not twisted:
            build_twist()
            twisted = True
        step(g)

    for g in range(chunks):
        for stage, ref, count in ((0, got1, coef_size - 1), (1, got3, limb_size - 1), (3, got5, coef_size - 1), (4, got7, limb_size - 1)):
            settle(ref.at[g, pl.ds(0, count)], ssem.at[stage, g])
        settle_back(got4.at[g], ssem.at[2, g], lift_block == chip)
        settle_back(got8.at[g], ssem.at[5, g], lower_block == chip)
    settle(got_t.at[pl.ds(0, coef_size - 1)], tsem.at[0])


def on_device(
    coef_size, limb_size,
    cipher_zero, cipher_one, key_main, key_special, lift_main, lift_special, lower_table, inverse_scale,
    inverse_main, inverse_special, forward_main, forward_special,
    inverse_rows, inverse_columns, forward_rows, forward_columns,
):
    ciphers = cipher_one.shape[0]
    chunks = ciphers // PART
    tile = (SUB, LANE)
    vmem = pl.BlockSpec(memory_space=pltpu.VMEM)
    small = (
        lift_main, lift_special.T, lower_table, inverse_scale, inverse_main, inverse_special, forward_main, forward_special,
        inverse_rows, inverse_columns, forward_rows, forward_columns,
    )
    out = jax.ShapeDtypeStruct((ciphers, 2, SUB, COLS), F32)
    item = pltpu.VMEM((chunks, coef_size) + tile, F32)
    depth = limb_size * SUB
    stages = 6
    zero, one = pl.pallas_call(
        functools.partial(kernel, coef_size, limb_size, chunks),
        out_shape=(out, out),
        in_specs=[vmem] * 4 + [pl.BlockSpec(memory_space=pltpu.HBM)] * len(small),
        out_specs=(vmem, vmem),
        scratch_shapes=[
            *(pltpu.SMEM(v.shape, F32) if v.ndim == 1 else pltpu.VMEM(v.shape, F32) for v in small),
            pltpu.SemaphoreType.DMA((len(small),)),
            item, item, item,
            pltpu.VMEM((chunks, limb_size, 2) + tile, F32),
            pltpu.VMEM((chunks, limb_size, 2, 3) + tile, F32),
            pltpu.VMEM((chunks, coef_size, 3) + tile, F32),
            item, item, item,
            pltpu.VMEM((chunks, limb_size, 2) + tile, F32),
            pltpu.VMEM((chunks, limb_size, 2, 2) + tile, F32),
            pltpu.VMEM((chunks, coef_size, 2) + tile, F32),
            pltpu.VMEM((coef_size,) + tile, F32),
            pltpu.VMEM((coef_size,) + tile, F32),
            pltpu.VMEM((3, 2) + tile, F32),
            pltpu.VMEM((chunks, PART, 2, 2 * SUB, COLS), F32),
            pltpu.VMEM((3 * COLS, COLS), BF16),
            pltpu.VMEM((3 * COLS, COLS), BF16),
            pltpu.VMEM((ROWS, 3 * ROWS), BF16),
            pltpu.VMEM((3 * depth, 3 * depth), BF16),
            pltpu.VMEM((2 * depth, 3 * depth), BF16),
            pltpu.SemaphoreType.DMA((stages, chunks)),
            pltpu.SemaphoreType.DMA((stages, chunks)),
            pltpu.SemaphoreType.DMA((2,)),
        ],
        compiler_params=pltpu.CompilerParams(
            collective_id=0, has_side_effects=True, vmem_limit_bytes=40 << 20
        ),
    )(
        cipher_one.reshape(ciphers, 2, SUB, COLS),
        cipher_zero.reshape(ciphers, 2, SUB, COLS),
        key_main.reshape(ciphers, 2, 2, 2 * SUB, COLS),
        key_special.reshape(ciphers, 2, 2 * SUB, COLS),
        *(pltpu.with_memory_space_constraint(v, pltpu.HBM) for v in small),
    )
    return zero.reshape(cipher_zero.shape), one.reshape(cipher_one.shape)


def solution(mesh):
    spread = P(None, "limb", "coef")
    keys = P(None, None, None, "limb", "coef")
    local = P("limb", "coef", None)
    placed = (spread, spread, keys, keys, P(), P(), P(), P("limb"), local, local, local, local, P(), P(), P(), P())
    return jax.shard_map(
        functools.partial(on_device, mesh.shape["coef"], mesh.shape["limb"]),
        mesh=mesh,
        in_specs=placed,
        out_specs=(spread, spread),
        check_vma=False,
    )
```

time: 130 us -> 181 us (1.39)
  the two profiles are of different devices: /device:TPU:2 before, /device:TPU:1 now
where the time goes in v1:
time: 181 us; the launch traced here: 179 us
  Pallas kernels  173 us (96%)
  local copies, waits for them, and re-layouts  4.97 us (3%)
    pallas_call x1, Pallas kernels, on_device(): pl.pallas_call(functools.partial(kernel, coef_size, limb_size, chunks), o...  173 us

profile of v1, /device:TPU:1, one launch (start us, length us, event | category | flops | bytes accessed | tf_op | source)
XLA Modules:
  0.0 178.9 jit_solution(15447215706382578943)
XLA Ops:
  0.6 0.0 copy-start.1
  0.6 0.0 copy-start.2
  0.6 1.4 reshape.23.zero_ref
  2.0 0.0 copy-done.1
  2.0 0.0 copy-start
  2.1 0.3 reshape.22.x_ref
  2.4 0.0 copy-done.2
  2.4 0.3 reshape.25.ks_ref
  2.6 0.5 copy-done
  3.2 0.5 reshape.24.km_ref
  3.7 173.2 %shard_map.167 = (f32[24,2,8,256]{3,2,1,0:T(8,128)S(1)}, f32[24,2,8,256]{3,2,1,0:T(8,128)S(1)}) custom-call(f32[24,2,8,256]{3,2,1,0:T(8,128)S(1)} %reshape.22.x_ref, f32[24,2,8,256]{3,2,1,0:T(8,128)S(1)} %reshape.23.zero_ref, bf16[24,2,2,16,256]{4,3,2,1,0:T(8,128)(2,1)S(1)} %reshape.24.km_ref, bf16[24,2,16,256]{3,2,1,0:T(8,128)(2,1)S(1)} %reshape.25.ks_ref, ...), custom_call_target="tpu_custom_call" | custom-call | tf_op jit(solution)/shard_map/pallas_call | solution.py:365
  176.9 1.0 reshape.26
  177.9 1.0 reshape.27
Async XLA Ops:
  0.6 1.4 copy-start.1
  0.6 1.7 copy-start.2
  2.0 1.1 copy-start

commit v2 on v0

--- a/solution.py
+++ b/solution.py
@@ -13,7 +13,7 @@
 ROWS = COLS = 256
 SUB, LANE = 8, 128
 PART = 8
-ORDER_SKEW = 1.0
+SMALL = ("lift_main", "lift_special", "lower", "scale", "tim", "tis", "tfm", "tfs", "ir", "ic", "fr", "fc")
 
 
 def halves(v):
@@ -59,11 +59,32 @@
 
 def kernel(
     coef_size, limb_size, chunks,
+    x_ref, zero_ref, km_ref, ks_ref, *rest,
+):
+    names = len(SMALL)
+    sources, (out0_ref, out1_ref) = rest[:names], rest[names:names + 2]
+    held, rest = rest[names + 2:2 * names + 2], rest[2 * names + 2:]
+    lsem, rest = rest[0], rest[1:]
+    loads = {
+        name: pltpu.make_async_copy(source, target, lsem.at[n])
+        for n, (name, source, target) in enumerate(zip(SMALL, sources, held))
+    }
+    for name in SMALL:
+        loads[name].start()
+    (lift_main_ref, lift_special_ref, lower_ref, scale_ref, tim_ref, tis_ref, tfm_ref, tfs_ref,
+     ir_ref, ic_ref, fr_ref, fc_ref) = held
+    body(coef_size, limb_size, chunks, loads, x_ref, zero_ref, km_ref, ks_ref,
+         lift_main_ref, lift_special_ref, lower_ref, scale_ref, tim_ref, tis_ref, tfm_ref, tfs_ref,
+         ir_ref, ic_ref, fr_ref, fc_ref, out0_ref, out1_ref, *rest)
+
+
+def body(
+    coef_size, limb_size, chunks, loads,
     x_ref, zero_ref, km_ref, ks_ref, lift_main_ref, lift_special_ref, lower_ref, scale_ref,
     tim_ref, tis_ref, tfm_ref, tfs_ref, ir_ref, ic_ref, fr_ref, fc_ref,
     out0_ref, out1_ref,
-    send1, got1, send2, got2, got3, send4, got4, send5, got5, send6, got6, got7, send8, got8,
-    send_t, got_t, twist, total, ic_w, fc_w, m_w, lift_w, lower_w,
+    send1, got1, send2, got2, got3, send_s, got_s, send_m, got_m, send5, got5, send6, got6, got7, send8, got8,
+    send_t, got_t, twist, total, ic_w, fc_w, m_w, special_w, main_w, lower_w,
     ssem, rsem, tsem,
 ):
     coef = lax.axis_index("coef")
@@ -82,6 +103,10 @@
     def _(j):
         pl.semaphore_signal(barrier, inc=1, device_id={"limb": lax.rem(limb + j, limb_size)}, device_id_type=MESH)
 
+    def need(*which):
+        for name in which:
+            loads[name].wait()
+
     def push(source, target, axis, peer, stage, g):
         pltpu.make_async_remote_copy(
             src_ref=source, dst_ref=target, send_sem=ssem.at[stage, g], recv_sem=rsem.at[stage, g],
@@ -131,15 +156,15 @@
 
         got3[g, place] = got2[g, pl.ds(4 * place, 4)]
 
-    def mixed(weight, got, send, stage, per, g, wait_count, wait_stage):
-        settle(got.at[g, pl.ds(0, wait_count)], rsem.at[wait_stage, g])
+    def mixed(weight, got, send, per, g):
         v = got[g].reshape(limb_size, 2, SUB, LANE)
-        both = jnp.concatenate(
-            [v[:, 0].reshape(limb_size * SUB, LANE), v[:, 1].reshape(limb_size * SUB, LANE)], axis=1
-        )
+        both = jnp.concatenate([v[:, h].reshape(limb_size * SUB, LANE) for h in range(2)], axis=1)
         w = fold(weight[...], data_columns(both)).reshape(limb_size, per, SUB, 2 * LANE)
         for h in range(2):
             send[g, :, :, h] = w[..., h * LANE:(h + 1) * LANE]
+
+    def limb_wait(got, stage, g, count=limb_size - 1):
+        settle(got.at[g, pl.ds(0, count)], rsem.at[stage, g])
 
     def limb_push(send, got, stage, g):
         @pl.loop(1, limb_size)
@@ -149,31 +174,39 @@
 
         got[g, limb] = send[g, limb]
 
-    def stage4(g):
-        mixed(lift_w, got3, send4, 3, 3, g, ring - 1, 2)
-        limb_push(send4, got4, 3, g)
-
-    def finish(v, kinds, n):
-        parts = [(v[:, :, h] * twist[:kinds, h][None]).reshape(n * kinds * SUB, LANE) for h in range(2)]
+    def stage4_special(g):
+        limb_wait(got3, 2, g, ring - 1)
+        mixed(special_w, got3, send_s, 1, g)
+        limb_push(send_s, got_s, 3, g)
+
+    def stage4_main(g):
+        mixed(main_w, got3, send_m, 2, g)
+        limb_push(send_m, got_m, 8, g)
+
+    def finish(v, scale):
+        n, kinds = v.shape[:2]
+        parts = [(v[:, :, h] * scale[:, h][None]).reshape(n * kinds * SUB, LANE) for h in range(2)]
         rows = jnp.concatenate(parts, axis=1)
         return fold(data_rows(rows), fc_w[...]).reshape(n, kinds * SUB, COLS)
 
     def stage5(g):
-        settle(got4.at[g, pl.ds(0, limb_size - 1)], rsem.at[3, g])
-        values = finish(got4[g], 3, limb_size).reshape(2, PART, 3 * SUB, COLS)
+        limb_wait(got_s, 3, g)
+        values = finish(got_s[g], twist[2:]).reshape(2, PART, SUB, COLS)
         here = pl.ds(PART * g, PART)
-        for i in range(2):
-            total[g, :, i] = sum(
-                values[d, :, :2 * SUB] * km_ref[here, d, i].astype(F32) for d in range(2)
-            )
-        special = 0.0
-        for d in range(2):
-            v = values[d, :, 2 * SUB:]
-            special = special + jnp.concatenate([v, v], axis=1) * ks_ref[here, d].astype(F32)
+        special = sum(
+            jnp.concatenate([values[d], values[d]], axis=1) * ks_ref[here, d].astype(F32) for d in range(2)
+        )
         a = fold(data_rows(special.reshape(PART * 2 * SUB, COLS)), ic_w[...])
         a = a.reshape(PART * 2, SUB, COLS) * tis_ref[...]
         to_items(send5, g, a)
         coef_push(send5, got5, 4, g)
+
+    def stage5_main(g):
+        limb_wait(got_m, 8, g)
+        values = finish(got_m[g], twist[:2]).reshape(2, PART, 2 * SUB, COLS)
+        here = pl.ds(PART * g, PART)
+        for i in range(2):
+            total[g, :, i] = sum(values[d] * km_ref[here, d, i].astype(F32) for d in range(2))
 
     def stage6(g):
         coef_wait(got5, 4, g)
@@ -192,12 +225,13 @@
         got7[g, limb] = got6[g, pl.ds(2 * limb, 2)]
 
     def stage8(g):
-        mixed(lower_w, got7, send8, 7, 2, g, limb_size - 1, 6)
+        limb_wait(got7, 6, g)
+        mixed(lower_w, got7, send8, 2, g)
         limb_push(send8, got8, 7, g)
 
     def stage9(g):
-        settle(got8.at[g, pl.ds(0, limb_size - 1)], rsem.at[7, g])
-        low = finish(got8[g], 2, limb_size).reshape(PART, 2, 2, SUB, COLS)
+        limb_wait(got8, 7, g)
+        low = finish(got8[g], twist[:2]).reshape(PART, 2, 2, SUB, COLS)
         here = pl.ds(PART * g, PART)
         for t in range(2):
             for i, out in enumerate((out0_ref, out1_ref)):
@@ -242,58 +276,48 @@
 
     def build_mixes():
         depth = limb_size * SUB
-        spread = selector((limb_size, depth), lambda s, c: c // SUB == s)
-        mine = pl.ds(pl.multiple_of(side * limb_size, SUB), limb_size)
-
-        def expand(table, rows):
+        kinds = limb_size * 2
+
+        def expand(table, spread):
+            rows = table.shape[0]
             wide = exact(table, spread, ((1,), (0,)))
             keep = lax.rem(iota((rows, depth), 0), SUB) == lax.rem(iota((rows, depth), 1), SUB)
             return weight_left(jnp.where(keep, wide, 0.0))
 
-        rows = limb_size * 3 * SUB
-        kinds = limb_size * 2
-
-        def main_of(r, t):
-            which = r // SUB
-            return (lax.rem(which, 3) < 2) & (2 * (which // 3) + lax.rem(which, 3) == t)
-
-        def special_of(r, u):
-            which = r // SUB
-            return (lax.rem(which, 3) == 2) & (which // 3 == u)
-
-        table = exact(selector((rows, kinds), main_of), lift_main_ref[mine], ((1,), (1,)))
-        table = table + exact(selector((rows, limb_size), special_of), lift_special_ref[mine], ((1,), (1,)))
-        lift_w[...] = expand(table, rows)
-        rows = kinds * SUB
-        table = exact(selector((rows, kinds), lambda r, t: r // SUB == t), lower_ref[...], ((1,), (1,)))
-        lower_w[...] = expand(table, rows)
-
+        pick = selector((kinds * SUB, kinds), lambda r, t: r // SUB == t)
+        mine = selector((kinds, depth), lambda s, c: c // SUB + side * limb_size == s)
+        table = exact(selector((depth, limb_size), lambda r, u: r // SUB == u), lift_special_ref[...], ((1,), (0,)))
+        special_w[...] = expand(table, mine)
+        main_w[...] = expand(exact(pick, lift_main_ref[...], ((1,), (1,))), mine)
+        table = exact(pick, lower_ref[...], ((1,), (1,)))
+        lower_w[...] = expand(table, selector((limb_size, depth), lambda s, c: c // SUB == s))
+
+    every = range(chunks)
+    need("ic", "tim")
     ic_w[...] = weight_right(ic_ref[...])
-    stage1(0)
+    for g in every:
+        stage1(g)
     pl.semaphore_wait(barrier, coef_size + limb_size - 2)
-    push1(0)
+    for g in every:
+        push1(g)
+    need("ir", "fr", "fc", "tfm", "tfs", "tis", "scale", "lift_main", "lift_special", "lower")
     build_weights()
+    for g in every:
+        stage2(g)
     prepare_twist()
-    for g in range(1, chunks):
-        stage1(g)
-        push1(g)
     push_twist()
     build_mixes()
-    work = []
-    for g in range(chunks):
-        for k, step in enumerate((stage2, stage3, stage4, stage5, stage6, stage7, stage8, stage9)):
-            work.append((k + ORDER_SKEW * g, g, k, step))
-    work.sort(key=lambda w: w[:3])
-    twisted = False
-    for _, g, k, step in work:
-        if k >= 2 and not twisted:
-            build_twist()
-            twisted = True
-        step(g)
+    for step in (stage3, stage4_special, stage4_main):
+        for g in every:
+            step(g)
+    build_twist()
+    for step in (stage5, stage6, stage7, stage8, stage5_main, stage9):
+        for g in every:
+            step(g)
 
     for g in range(chunks):
         for stage, ref, count in (
-            (0, got1, coef_size - 1), (1, got2, coef_size - 1), (2, got3, ring - 1), (3, got4, limb_size - 1),
+            (0, got1, coef_size - 1), (1, got2, coef_size - 1), (2, got3, ring - 1), (3, got_s, limb_size - 1), (8, got_m, limb_size - 1),
             (4, got5, coef_size - 1), (5, got6, coef_size - 1), (6, got7, limb_size - 1), (7, got8, limb_size - 1),
         ):
             settle(ref.at[g, pl.ds(0, count)], ssem.at[stage, g])
@@ -310,21 +334,28 @@
     chunks = ciphers // PART
     tile = (SUB, LANE)
     vmem = pl.BlockSpec(memory_space=pltpu.VMEM)
-    smem = pl.BlockSpec(memory_space=pltpu.SMEM)
+    small = (
+        lift_main, lift_special.T, lower_table, inverse_scale, inverse_main, inverse_special, forward_main, forward_special,
+        inverse_rows, inverse_columns, forward_rows, forward_columns,
+    )
     out = jax.ShapeDtypeStruct((ciphers, 2, SUB, COLS), F32)
     item = pltpu.VMEM((chunks, coef_size) + tile, F32)
     depth = limb_size * SUB
-    stages = 8
+    stages = 9
     zero, one = pl.pallas_call(
         functools.partial(kernel, coef_size, limb_size, chunks),
         out_shape=(out, out),
-        in_specs=[vmem] * 7 + [smem] + [vmem] * 8,
+        in_specs=[vmem] * 4 + [pl.BlockSpec(memory_space=pltpu.HBM)] * len(small),
         out_specs=(vmem, vmem),
         scratch_shapes=[
+            *(pltpu.SMEM(v.shape, F32) if v.ndim == 1 else pltpu.VMEM(v.shape, F32) for v in small),
+            pltpu.SemaphoreType.DMA((len(small),)),
             item, item, item, item,
             pltpu.VMEM((chunks, limb_size // 2, 4) + tile, F32),
-            pltpu.VMEM((chunks, limb_size, 3, 2) + tile, F32),
-            pltpu.VMEM((chunks, limb_size, 3, 2) + tile, F32),
+            pltpu.VMEM((chunks, limb_size, 1, 2) + tile, F32),
+            pltpu.VMEM((chunks, limb_size, 1, 2) + tile, F32),
+            pltpu.VMEM((chunks, limb_size, 2, 2) + tile, F32),
+            pltpu.VMEM((chunks, limb_size, 2, 2) + tile, F32),
             item, item, item, item,
             pltpu.VMEM((chunks, limb_size, 2) + tile, F32),
             pltpu.VMEM((chunks, limb_size, 2, 2) + tile, F32),
@@ -336,7 +367,8 @@
             pltpu.VMEM((3 * COLS, COLS), BF16),
             pltpu.VMEM((3 * COLS, COLS), BF16),
             pltpu.VMEM((ROWS, 3 * ROWS), BF16),
-            pltpu.VMEM((3 * depth, 3 * depth), BF16),
+            pltpu.VMEM((depth, 3 * depth), BF16),
+            pltpu.VMEM((2 * depth, 3 * depth), BF16),
             pltpu.VMEM((2 * depth, 3 * depth), BF16),
             pltpu.SemaphoreType.DMA((stages, chunks)),
             pltpu.SemaphoreType.DMA((stages, chunks)),
@@ -350,9 +382,7 @@
         cipher_zero.reshape(ciphers, 2, SUB, COLS),
         key_main.reshape(ciphers, 2, 2, 2 * SUB, COLS),
         key_special.reshape(ciphers, 2, 2 * SUB, COLS),
-        lift_main, lift_special, lower_table, inverse_scale,
-        inverse_main, inverse_special, forward_main, forward_special,
-        inverse_rows, inverse_columns, forward_rows, forward_columns,
+        *(pltpu.with_memory_space_constraint(v, pltpu.HBM) for v in small),
     )
     return zero.reshape(cipher_zero.shape), one.reshape(cipher_one.shape)
 

time: 130 us -> 101 us (0.78)
  the two profiles are of different devices: /device:TPU:2 before, /device:TPU:1 now
where the time goes in v2:
time: 101 us
  Pallas kernels  95.6 us (95%)
  local copies, waits for them, and re-layouts  4.97 us (5%)
    pallas_call x1, Pallas kernels, on_device(): pl.pallas_call(functools.partial(kernel, coef_size, limb_size, chunks), o...  95.6 us

profile of v2, /device:TPU:1, one launch (start us, length us, event | category | flops | bytes accessed | tf_op | source)
XLA Modules:
  0.0 101.3 jit_solution(3476529039114421621)
XLA Ops:
  0.6 0.0 copy-start.1
  0.6 0.0 copy-start.2
  0.6 1.4 %reshape.23.zero_ref = f32[24,2,8,256]{3,2,1,0:T(8,128)S(1)} reshape(f32[24,2,2048]{2,1,0:T(2,128)} %param.16) | data formatting | bytes 786432 | tf_op jit(solution)/shard_map/reshape | solution.py:382
  2.0 0.0 copy-done.1
  2.0 0.0 copy-start
  2.1 0.3 reshape.22.x_ref
  2.4 0.0 copy-done.2
  2.4 0.3 reshape.25.ks_ref
  2.6 0.5 copy-done
  3.2 0.5 reshape.24.km_ref
  3.7 95.6 %shard_map.167 = (f32[24,2,8,256]{3,2,1,0:T(8,128)S(1)}, f32[24,2,8,256]{3,2,1,0:T(8,128)S(1)}) custom-call(f32[24,2,8,256]{3,2,1,0:T(8,128)S(1)} %reshape.22.x_ref, f32[24,2,8,256]{3,2,1,0:T(8,128)S(1)} %reshape.23.zero_ref, bf16[24,2,2,16,256]{4,3,2,1,0:T(8,128)(2,1)S(1)} %reshape.24.km_ref, bf16[24,2,16,256]{3,2,1,0:T(8,128)(2,1)S(1)} %reshape.25.ks_ref, ...), custom_call_target="tpu_custom_call" | custom-call | tf_op jit(solution)/shard_map/pallas_call | solution.py:345
  99.3 1.0 reshape.26
  100.3 1.0 reshape.27
Async XLA Ops:
  0.6 1.4 %copy-start.1 = (f32[24,2,2048]{2,1,0:T(2,128)S(1)}, f32[24,2,2048]{2,1,0:T(2,128)}, u32[]{:S(2)}) copy-start(f32[24,2,2048]{2,1,0:T(2,128)} %param.17) | copy-start | bytes 1179652
  0.6 1.7 %copy-start.2 = (bf16[24,2,2,1,2048]{4,2,3,1,0:T(2,128)(2,1)S(1)}, bf16[24,2,2,1,2048]{4,2,3,1,0:T(2,128)(2,1)}, u32[]{:S(2)}) copy-start(bf16[24,2,2,1,2048]{4,2,3,1,0:T(2,128)(2,1)} %param.19) | copy-start | bytes 1179652
  2.0 1.1 %copy-start = (bf16[24,2,2,2,2048]{4,3,2,1,0:T(2,128)(2,1)S(1)}, bf16[24,2,2,2,2048]{4,3,2,1,0:T(2,128)(2,1)}, u32[]{:S(2)}) copy-start(bf16[24,2,2,2,2048]{4,3,2,1,0:T(2,128)(2,1)} %param.18) | copy-start | bytes 2359300

commit v3 on v2

--- a/solution.py
+++ b/solution.py
@@ -59,7 +59,7 @@
 
 def kernel(
     coef_size, limb_size, chunks,
-    x_ref, zero_ref, km_ref, ks_ref, *rest,
+    x_ref, km_ref, ks_ref, *rest,
 ):
     names = len(SMALL)
     sources, (out0_ref, out1_ref) = rest[:names], rest[names:names + 2]
@@ -69,18 +69,18 @@
         name: pltpu.make_async_copy(source, target, lsem.at[n])
         for n, (name, source, target) in enumerate(zip(SMALL, sources, held))
     }
-    for name in SMALL:
+    for name in ("ic", "tim") + tuple(n for n in SMALL if n not in ("ic", "tim")):
         loads[name].start()
     (lift_main_ref, lift_special_ref, lower_ref, scale_ref, tim_ref, tis_ref, tfm_ref, tfs_ref,
      ir_ref, ic_ref, fr_ref, fc_ref) = held
-    body(coef_size, limb_size, chunks, loads, x_ref, zero_ref, km_ref, ks_ref,
+    body(coef_size, limb_size, chunks, loads, x_ref, km_ref, ks_ref,
          lift_main_ref, lift_special_ref, lower_ref, scale_ref, tim_ref, tis_ref, tfm_ref, tfs_ref,
          ir_ref, ic_ref, fr_ref, fc_ref, out0_ref, out1_ref, *rest)
 
 
 def body(
     coef_size, limb_size, chunks, loads,
-    x_ref, zero_ref, km_ref, ks_ref, lift_main_ref, lift_special_ref, lower_ref, scale_ref,
+    x_ref, km_ref, ks_ref, lift_main_ref, lift_special_ref, lower_ref, scale_ref,
     tim_ref, tis_ref, tfm_ref, tfs_ref, ir_ref, ic_ref, fr_ref, fc_ref,
     out0_ref, out1_ref,
     send1, got1, send2, got2, got3, send_s, got_s, send_m, got_m, send5, got5, send6, got6, got7, send8, got8,
@@ -116,10 +116,20 @@
     def settle(ref, sem):
         pltpu.make_async_copy(ref, ref, sem).wait()
 
+    tall = coef_size // 4
+    chip = coef // 2
+
+    def far_first(j):
+        m = j // 4
+        odd = lax.rem(m, 2)
+        up = odd * (tall // 2 - 1 - m // 2) + (1 - odd) * (tall // 2 + m // 2)
+        across = lax.rem(chip // tall + 1 - lax.rem(j // 2, 2), 2)
+        return (across * tall + lax.rem(lax.rem(chip, tall) + up, tall)) * 2 + lax.rem(coef + 1 - lax.rem(j, 2), 2)
+
     def coef_push(send, got, stage, g):
-        @pl.loop(1, coef_size)
+        @pl.loop(0, coef_size - 1)
         def _(j):
-            peer = lax.rem(coef + j, coef_size)
+            peer = far_first(j)
             push(send.at[g, peer], got.at[g, coef], "coef", peer, stage, g)
 
         got[g, coef] = send[g, coef]
@@ -235,8 +245,7 @@
         here = pl.ds(PART * g, PART)
         for t in range(2):
             for i, out in enumerate((out0_ref, out1_ref)):
-                result = scale_ref[t] * (total[g, :, i, t * SUB:(t + 1) * SUB] - low[:, i, t])
-                out[here, t] = zero_ref[here, t] + result if i == 0 else result
+                out[here, t] = scale_ref[t] * (total[g, :, i, t * SUB:(t + 1) * SUB] - low[:, i, t])
 
     def prepare_twist():
         rows = jnp.concatenate(
@@ -302,12 +311,14 @@
         push1(g)
     need("ir", "fr", "fc", "tfm", "tfs", "tis", "scale", "lift_main", "lift_special", "lower")
     build_weights()
+    build_mixes()
+    prepare_twist()
     for g in every:
         stage2(g)
-    prepare_twist()
+    for g in every:
+        stage3(g)
     push_twist()
-    build_mixes()
-    for step in (stage3, stage4_special, stage4_main):
+    for step in (stage4_special, stage4_main):
         for g in every:
             step(g)
     build_twist()
@@ -345,7 +356,7 @@
     zero, one = pl.pallas_call(
         functools.partial(kernel, coef_size, limb_size, chunks),
         out_shape=(out, out),
-        in_specs=[vmem] * 4 + [pl.BlockSpec(memory_space=pltpu.HBM)] * len(small),
+        in_specs=[vmem] * 3 + [pl.BlockSpec(memory_space=pltpu.HBM)] * len(small),
         out_specs=(vmem, vmem),
         scratch_shapes=[
             *(pltpu.SMEM(v.shape, F32) if v.ndim == 1 else pltpu.VMEM(v.shape, F32) for v in small),
@@ -379,12 +390,11 @@
         ),
     )(
         cipher_one.reshape(ciphers, 2, SUB, COLS),
-        cipher_zero.reshape(ciphers, 2, SUB, COLS),
         key_main.reshape(ciphers, 2, 2, 2 * SUB, COLS),
         key_special.reshape(ciphers, 2, 2 * SUB, COLS),
         *(pltpu.with_memory_space_constraint(v, pltpu.HBM) for v in small),
     )
-    return zero.reshape(cipher_zero.shape), one.reshape(cipher_one.shape)
+    return cipher_zero + zero.reshape(cipher_zero.shape), one.reshape(cipher_one.shape)
 
 
 def solution(mesh):

time: 101 us -> 100 us (0.990)
  Pallas kernels: 95.6 us -> 93.4 us
    pallas_call x1, Pallas kernels: 95.6 us -> 93.4 us  [on_device(): pl.pallas_call(functools.partial(kernel, coef_size, limb_size, chunks), o...]
    reshape x3 -> x2, local copies, waits for them, and re-layouts: 3.36 us -> 1.25 us  [the longest x1 0.99 us: on_device(): one.reshape(cipher_one.shape)]
    reshape x1, local copies, waits for them, and re-layouts: 0.32 us -> 1.38 us  [on_device(): cipher_one.reshape(ciphers, 2, SUB, COLS)]
where the time goes in v3:
time: 100 us
  Pallas kernels  93.4 us (93%)
  local copies, waits for them, and re-layouts  5.11 us (5%)
    pallas_call x1, Pallas kernels, on_device(): pl.pallas_call(functools.partial(kernel, coef_size, limb_size, chunks), o...  93.4 us

profile of v3, /device:TPU:1, one launch (start us, length us, event | category | flops | bytes accessed | tf_op | source)
XLA Modules:
  0.0 100.1 jit_solution(17138979838058754626)
XLA Ops:
  0.6 0.0 copy-start
  0.6 1.4 %reshape.19.x_ref = f32[24,2,8,256]{3,2,1,0:T(8,128)S(1)} reshape(f32[24,2,2048]{2,1,0:T(2,128)} %param.17) | data formatting | bytes 786432 | tf_op jit(solution)/shard_map/reshape | solution.py:392
  2.0 1.2 %reshape.21.ks_ref = bf16[24,2,16,256]{3,2,1,0:T(8,128)(2,1)S(1)} reshape(bf16[24,2,2,1,2048]{4,2,3,1,0:T(2,128)(2,1)} %param.19) | data formatting | bytes 786432 | tf_op jit(solution)/shard_map/reshape | solution.py:394
  3.3 0.0 copy-done
  3.3 0.5 reshape.20.km_ref
  3.8 93.4 %shard_map.167 = (f32[24,2,8,256]{3,2,1,0:T(8,128)S(1)}, f32[24,2,8,256]{3,2,1,0:T(8,128)S(1)}) custom-call(f32[24,2,8,256]{3,2,1,0:T(8,128)S(1)} %reshape.19.x_ref, bf16[24,2,2,16,256]{4,3,2,1,0:T(8,128)(2,1)S(1)} %reshape.20.km_ref, bf16[24,2,16,256]{3,2,1,0:T(8,128)(2,1)S(1)} %reshape.21.ks_ref, f32[32,32]{1,0:T(8,128)} %rest_0_.1, f32[16,32]{1,0:T(8,128)} %bitcast.7, ...), custom_call_target="tpu_custom_call" | custom-call | tf_op jit(solution)/shard_map/pallas_call | solution.py:356
  97.2 0.0 copy-start.1
  97.2 0.3 reshape.22
  97.4 0.7 copy-done.1
  98.2 1.0 add.3
  99.1 1.0 reshape.23
Async XLA Ops:
  0.6 2.7 %copy-start = (bf16[24,2,2,2,2048]{4,3,2,1,0:T(2,128)(2,1)S(1)}, bf16[24,2,2,2,2048]{4,3,2,1,0:T(2,128)(2,1)}, u32[]{:S(2)}) copy-start(bf16[24,2,2,2,2048]{4,3,2,1,0:T(2,128)(2,1)} %param.18) | copy-start | bytes 2359300
  97.2 1.0 copy-start.1

commit v4 on v3

--- a/solution.py
+++ b/solution.py
@@ -59,7 +59,7 @@
 
 def kernel(
     coef_size, limb_size, chunks,
-    x_ref, km_ref, ks_ref, *rest,
+    x_ref, zero_ref, km_ref, ks_ref, *rest,
 ):
     names = len(SMALL)
     sources, (out0_ref, out1_ref) = rest[:names], rest[names:names + 2]
@@ -73,14 +73,14 @@
         loads[name].start()
     (lift_main_ref, lift_special_ref, lower_ref, scale_ref, tim_ref, tis_ref, tfm_ref, tfs_ref,
      ir_ref, ic_ref, fr_ref, fc_ref) = held
-    body(coef_size, limb_size, chunks, loads, x_ref, km_ref, ks_ref,
+    body(coef_size, limb_size, chunks, loads, x_ref, zero_ref, km_ref, ks_ref,
          lift_main_ref, lift_special_ref, lower_ref, scale_ref, tim_ref, tis_ref, tfm_ref, tfs_ref,
          ir_ref, ic_ref, fr_ref, fc_ref, out0_ref, out1_ref, *rest)
 
 
 def body(
     coef_size, limb_size, chunks, loads,
-    x_ref, km_ref, ks_ref, lift_main_ref, lift_special_ref, lower_ref, scale_ref,
+    x_ref, zero_ref, km_ref, ks_ref, lift_main_ref, lift_special_ref, lower_ref, scale_ref,
     tim_ref, tis_ref, tfm_ref, tfs_ref, ir_ref, ic_ref, fr_ref, fc_ref,
     out0_ref, out1_ref,
     send1, got1, send2, got2, got3, send_s, got_s, send_m, got_m, send5, got5, send6, got6, got7, send8, got8,
@@ -245,7 +245,8 @@
         here = pl.ds(PART * g, PART)
         for t in range(2):
             for i, out in enumerate((out0_ref, out1_ref)):
-                out[here, t] = scale_ref[t] * (total[g, :, i, t * SUB:(t + 1) * SUB] - low[:, i, t])
+                result = scale_ref[t] * (total[g, :, i, t * SUB:(t + 1) * SUB] - low[:, i, t])
+                out[here, t] = zero_ref[here, t] + result if i == 0 else result
 
     def prepare_twist():
         rows = jnp.concatenate(
@@ -356,7 +357,7 @@
     zero, one = pl.pallas_call(
         functools.partial(kernel, coef_size, limb_size, chunks),
         out_shape=(out, out),
-        in_specs=[vmem] * 3 + [pl.BlockSpec(memory_space=pltpu.HBM)] * len(small),
+        in_specs=[vmem] * 4 + [pl.BlockSpec(memory_space=pltpu.HBM)] * len(small),
         out_specs=(vmem, vmem),
         scratch_shapes=[
             *(pltpu.SMEM(v.shape, F32) if v.ndim == 1 else pltpu.VMEM(v.shape, F32) for v in small),
@@ -390,11 +391,12 @@
         ),
     )(
         cipher_one.reshape(ciphers, 2, SUB, COLS),
+        cipher_zero.reshape(ciphers, 2, SUB, COLS),
         key_main.reshape(ciphers, 2, 2, 2 * SUB, COLS),
         key_special.reshape(ciphers, 2, 2 * SUB, COLS),
         *(pltpu.with_memory_space_constraint(v, pltpu.HBM) for v in small),
     )
-    return cipher_zero + zero.reshape(cipher_zero.shape), one.reshape(cipher_one.shape)
+    return zero.reshape(cipher_zero.shape), one.reshape(cipher_one.shape)
 
 
 def solution(mesh):

time: 100 us -> 99.3 us (level)
    reshape x2 -> x3, local copies, waits for them, and re-layouts: 1.25 us -> 3.36 us  [the longest x2 1.98 us: on_device(): return (zero.reshape(cipher_zero.shape), one.reshape(cipher_one.shape))]
    reshape x1, local copies, waits for them, and re-layouts: 1.38 us -> 0.32 us  [on_device(): cipher_one.reshape(ciphers, 2, SUB, COLS)]
where the time goes in v4:
time: 99.3 us; the launch traced here: 99.1 us
  Pallas kernels  93.4 us (94%)
  local copies, waits for them, and re-layouts  4.97 us (5%)
    pallas_call x1, Pallas kernels, on_device(): pl.pallas_call(functools.partial(kernel, coef_size, limb_size, chunks), o...  93.4 us

profile of v4, /device:TPU:1, one launch (start us, length us, event | category | flops | bytes accessed | tf_op | source)
XLA Modules:
  0.0 99.1 jit_solution(2430602345512240283)
XLA Ops:
  0.6 0.0 copy-start.1
  0.6 0.0 copy-start.2
  0.6 1.4 %reshape.23.zero_ref = f32[24,2,8,256]{3,2,1,0:T(8,128)S(1)} reshape(f32[24,2,2048]{2,1,0:T(2,128)} %param.16) | data formatting | bytes 786432 | tf_op jit(solution)/shard_map/reshape | solution.py:394
  2.0 0.0 copy-done.1
  2.0 0.0 copy-start
  2.1 0.3 reshape.22.x_ref
  2.4 0.0 copy-done.2
  2.4 0.3 reshape.25.ks_ref
  2.6 0.5 copy-done
  3.2 0.5 reshape.24.km_ref
  3.7 93.4 %shard_map.167 = (f32[24,2,8,256]{3,2,1,0:T(8,128)S(1)}, f32[24,2,8,256]{3,2,1,0:T(8,128)S(1)}) custom-call(f32[24,2,8,256]{3,2,1,0:T(8,128)S(1)} %reshape.22.x_ref, f32[24,2,8,256]{3,2,1,0:T(8,128)S(1)} %reshape.23.zero_ref, bf16[24,2,2,16,256]{4,3,2,1,0:T(8,128)(2,1)S(1)} %reshape.24.km_ref, bf16[24,2,16,256]{3,2,1,0:T(8,128)(2,1)S(1)} %reshape.25.ks_ref, ...), custom_call_target="tpu_custom_call" | custom-call | tf_op jit(solution)/shard_map/pallas_call | solution.py:357
  97.1 1.0 %reshape.26 = f32[24,2,2048]{2,1,0:T(2,128)} reshape(f32[24,2,8,256]{3,2,1,0:T(8,128)S(1)} %get-tuple-element.4) | data formatting | bytes 786432 | tf_op jit(solution)/shard_map/reshape | solution.py:399
  98.1 1.0 reshape.27
Async XLA Ops:
  0.6 1.4 %copy-start.1 = (f32[24,2,2048]{2,1,0:T(2,128)S(1)}, f32[24,2,2048]{2,1,0:T(2,128)}, u32[]{:S(2)}) copy-start(f32[24,2,2048]{2,1,0:T(2,128)} %param.17) | copy-start | bytes 1179652
  0.6 1.7 %copy-start.2 = (bf16[24,2,2,1,2048]{4,2,3,1,0:T(2,128)(2,1)S(1)}, bf16[24,2,2,1,2048]{4,2,3,1,0:T(2,128)(2,1)}, u32[]{:S(2)}) copy-start(bf16[24,2,2,1,2048]{4,2,3,1,0:T(2,128)(2,1)} %param.19) | copy-start | bytes 1179652
  2.0 1.1 %copy-start = (bf16[24,2,2,2,2048]{4,3,2,1,0:T(2,128)(2,1)S(1)}, bf16[24,2,2,2,2048]{4,3,2,1,0:T(2,128)(2,1)}, u32[]{:S(2)}) copy-start(bf16[24,2,2,2,2048]{4,3,2,1,0:T(2,128)(2,1)} %param.18) | copy-start | bytes 2359300
